TPU v7x, 32 devices: a whole 2x2x4 slice. The times are simulated.
32 devices in a mesh: samp: 8 (over z, x), state: 4 (over y, core).
Axes of the slice: x: 2, y: 2, z: 4, core: 2. Of those that a mesh axis runs over, the one named last changes fastest.
Arguments:
- energies: bfloat16 [4096, 131072], P('state', 'samp'), may hold values from -12 to 12
- offsets: float32 [4096, 1024], P('state', 'samp'), may hold values from -250 to 250
- counts: int32 [4096], P('state'), may hold values from 1 to 31745, as said below
- labels: int32 [131072], P('samp'), may hold values from 0 to 4095
Outputs:
- free_energy: float32 [4096], P('state')
- own_log_probability: float32 [131072], P('samp')
Inputs may be any that keep to these rules, and one draw needn't show every extreme that they name: counts[k] is the number of samples n with labels[n] = k; every state has a sample, state 4096 - 1 has exactly one, and state 0 has the most.
All inputs are finite; a program needn't handle non-finite values.
Results may differ from a plain program's by a relative error of at most 0.0003.
Values sent between devices are 32-bit elements; how exact they have to be, the bound alone decides.
A program may use at most 256 MiB of HBM per device.

v0:
```python
import jax
import jax.numpy as jnp
from jax import lax
from jax.sharding import PartitionSpec as P

ITERS = 3


def from_root(value, axis, root):
    mine = lax.axis_index(axis) == root
    return lax.psum(jnp.where(mine, value, jnp.zeros_like(value)), axis)


def local_energy(energies, offsets):
    rows, width = energies.shape
    nblk = offsets.shape[1]
    shaped = energies.astype(jnp.float32).reshape(rows, nblk, width // nblk)
    return (shaped + offsets[:, :, None]).reshape(rows, width)


def sample_denominator(energies, offsets, lead):
    terms = lead[:, None] - local_energy(energies, offsets)
    width = terms.shape[1]
    best = jnp.max(terms, axis=0)
    total = jnp.sum(jnp.exp(terms - best[None, :]), axis=0)
    groups = lax.axis_size("state")
    parts = (
        lax.all_to_all(
            best.reshape(groups, width // groups), "state", split_axis=0, concat_axis=0, tiled=True
        ),
        lax.all_to_all(
            total.reshape(groups, width // groups), "state", split_axis=0, concat_axis=0, tiled=True
        ),
    )
    peak = jnp.max(parts[0], axis=0)
    whole = jnp.sum(parts[1] * jnp.exp(parts[0] - peak[None, :]), axis=0)
    return lax.all_gather(peak + jnp.log(whole), "state", axis=0, tiled=True)


def state_update(energies, offsets, denom):
    terms = -local_energy(energies, offsets) - denom[None, :]
    best = lax.pmax(jnp.max(terms, axis=1), "samp")
    total = lax.psum(jnp.sum(jnp.exp(terms - best[:, None]), axis=1), "samp")
    return -(best + jnp.log(total))


def own_terms_local(energies, offsets, lead, local_label):
    rows, width = energies.shape
    nblk = offsets.shape[1]
    block_size = width // nblk
    span = min(width, max(block_size, 512))
    span = span - span % block_size
    while width % span != 0:
        span = span - block_size
    steps_count = width // span
    row_ids = jnp.arange(rows, dtype=jnp.int32)

    def one(index):
        start = index * span
        part = lax.dynamic_slice_in_dim(energies, start, span, 1).astype(jnp.float32)
        shift = lax.dynamic_slice_in_dim(
            offsets, index * (span // block_size), span // block_size, 1
        )
        energy_part = (
            part.reshape(rows, span // block_size, block_size) + shift[:, :, None]
        ).reshape(rows, span)
        wanted = lax.dynamic_slice_in_dim(local_label, start, span, 0)
        match = row_ids[:, None] == wanted[None, :]
        return jnp.sum(jnp.where(match, lead[:, None] - energy_part, 0.0), axis=0)

    return lax.map(one, jnp.arange(steps_count, dtype=jnp.int32)).reshape(width)


def shards(energies, offsets, counts, labels):
    rows, width = energies.shape
    logc = jnp.log(counts.astype(jnp.float32))
    free = jnp.zeros((rows,), jnp.float32)
    for step in range(ITERS):
        denom = sample_denominator(energies, offsets, logc + free)
        free = state_update(energies, offsets, denom)
    lead = logc + free
    denom = sample_denominator(energies, offsets, lead)
    local_label = labels - lax.axis_index("state") * rows
    picked = own_terms_local(energies, offsets, lead, local_label)
    own = lax.psum(picked, "state") - denom
    anchor_value = from_root(free[0:1], "state", 0)
    return (free - anchor_value[0], own)


def solution(mesh):
    return jax.shard_map(
        shards,
        mesh=mesh,
        in_specs=(P("state", "samp"), P("state", "samp"), P("state"), P("samp")),
        out_specs=(P("state"), P("samp")),
        check_vma=False,
    )
```

profile of v0, /device:TPU:0, one launch (start us, length us, event | category | flops | bytes accessed | tf_op | source)
XLA Modules:
  0.0 765.3 jit_solution(17431815662996339874)
XLA Ops:
  7.9 22.2 %add.48 = f32[1024,128,128]{2,1,0:T(8,128)} broadcast(f32[1024,128]{1,0:T(8,128)} %param.7), dimensions={0,1} | broadcast | bytes 67633152 | tf_op jit(solution)/shard_map/add | solution.py:18
  30.0 74.5 %subtract_reduce_fusion.6 = (f32[16384]{0:T(1024)}, f32[1024,16384]{1,0:T(8,128)}) fusion(f32[1024]{0:T(1024)S(1)} %convert_log_fusion, f32[128,8,128,128]{3,2,1,0:T(8,128)} %bitcast.23, bf16[1024,16384]{1,0:T(8,128)(2,1)} %param.6), kind=kLoop, calls=%fused_computation.21 | loop fusion | flops 67092480 | bytes 167841792 | tf_op jit(solution)/shard_map/reduce_max | solution.py:24
  108.8 24.4 %exponential_reduce_fusion.6 = f32[16384]{0:T(1024)} fusion(f32[1024,16384]{1,0:T(8,128)} %get-tuple-element.78, f32[16384]{0:T(1024)} %get-tuple-element.77, f32[1024]{0:T(1024)S(1)} %convert_log_fusion), kind=kLoop, calls=%fused_computation.14 | loop fusion | flops 50315264 | bytes 67244032 | tf_op jit(solution)/shard_map/reduce_sum | solution.py:25
  146.0 21.0 %subtract_reduce_fusion.5 = f32[1024]{0:T(1024)S(1)} fusion(f32[1024,16384]{1,0:T(8,128)} %get-tuple-element.78, f32[16384]{0:T(1024)S(1)} %all_gather.12), kind=kLoop, calls=%fused_computation.20 | loop fusion | flops 50330624 | bytes 67178496 | tf_op jit(solution)/shard_map/reduce_max | solution.py:42
  167.0 22.1 %pmax.21 = f32[1024]{0:T(1024)S(1)} all-reduce(f32[1024]{0:T(1024)S(1)} %subtract_reduce_fusion.5), channel_id=1, replica_groups=mesh['samp'=8,'state'=4] {'samp'}, use_global_device_ids=true, to_apply=%region_5.0 | all-reduce | flops 1024 | bytes 8192 | tf_op jit(solution)/shard_map/pmax | solution.py:42
  189.1 21.4 %exponential_reduce_fusion.5 = f32[1024]{0:T(1024)S(1)} fusion(f32[1024,16384]{1,0:T(8,128)} %get-tuple-element.78, f32[1024]{0:T(1024)S(1)} %pmax.21, f32[16384]{0:T(1024)S(1)} %all_gather.12), kind=kLoop, calls=%fused_computation.13 | loop fusion | flops 67107840 | bytes 67182592 | tf_op jit(solution)/shard_map/reduce_sum | solution.py:43
  210.5 17.1 %psum.35 = f32[1024]{0:T(1024)S(1)} all-reduce(f32[1024]{0:T(1024)S(1)} %exponential_reduce_fusion.5), channel_id=1, replica_groups=mesh['samp'=8,'state'=4] {'samp'}, use_global_device_ids=true, to_apply=%region_7.0 | all-reduce | flops 1024 | bytes 8192 | tf_op jit(solution)/shard_map/psum | solution.py:43
  227.7 21.5 %subtract_reduce_fusion.4 = f32[16384]{0:T(1024)} fusion(f32[1024,16384]{1,0:T(8,128)} %get-tuple-element.78, f32[1024]{0:T(1024)S(1)} %negate_add_fusion.1), kind=kLoop, calls=%fused_computation.19 | loop fusion | flops 33538048 | bytes 67178496 | tf_op jit(solution)/shard_map/reduce_max | solution.py:24
  252.4 24.4 %exponential_reduce_fusion.4 = f32[16384]{0:T(1024)} fusion(f32[1024,16384]{1,0:T(8,128)} %get-tuple-element.78, f32[16384]{0:T(1024)} %subtract_reduce_fusion.4, f32[1024]{0:T(1024)S(1)} %negate_add_fusion.1), kind=kLoop, calls=%fused_computation.12 | loop fusion | flops 50315264 | bytes 67244032 | tf_op jit(solution)/shard_map/reduce_sum | solution.py:25
  289.6 21.0 %subtract_reduce_fusion.3 = f32[1024]{0:T(1024)S(1)} fusion(f32[1024,16384]{1,0:T(8,128)} %get-tuple-element.78, f32[16384]{0:T(1024)S(1)} %all_gather.13), kind=kLoop, calls=%fused_computation.18 | loop fusion | flops 50330624 | bytes 67178496 | tf_op jit(solution)/shard_map/reduce_max | solution.py:42
  310.7 19.3 %pmax.22 = f32[1024]{0:T(1024)S(1)} all-reduce(f32[1024]{0:T(1024)S(1)} %subtract_reduce_fusion.3), channel_id=1, replica_groups=mesh['samp'=8,'state'=4] {'samp'}, use_global_device_ids=true, to_apply=%region_13.0 | all-reduce | flops 1024 | bytes 8192 | tf_op jit(solution)/shard_map/pmax | solution.py:42
  330.0 21.4 %exponential_reduce_fusion.3 = f32[1024]{0:T(1024)S(1)} fusion(f32[1024,16384]{1,0:T(8,128)} %get-tuple-element.78, f32[1024]{0:T(1024)S(1)} %pmax.22, f32[16384]{0:T(1024)S(1)} %all_gather.13), kind=kLoop, calls=%fused_computation.11 | loop fusion | flops 67107840 | bytes 67182592 | tf_op jit(solution)/shard_map/reduce_sum | solution.py:43
  351.3 17.1 %psum.36 = f32[1024]{0:T(1024)S(1)} all-reduce(f32[1024]{0:T(1024)S(1)} %exponential_reduce_fusion.3), channel_id=1, replica_groups=mesh['samp'=8,'state'=4] {'samp'}, use_global_device_ids=true, to_apply=%region_15.0 | all-reduce | flops 1024 | bytes 8192 | tf_op jit(solution)/shard_map/psum | solution.py:43
  368.5 21.5 %subtract_reduce_fusion.2 = f32[16384]{0:T(1024)} fusion(f32[1024,16384]{1,0:T(8,128)} %get-tuple-element.78, f32[1024]{0:T(1024)S(1)} %negate_add_fusion), kind=kLoop, calls=%fused_computation.17 | loop fusion | flops 33538048 | bytes 67178496 | tf_op jit(solution)/shard_map/reduce_max | solution.py:24
  393.3 24.4 %exponential_reduce_fusion.2 = f32[16384]{0:T(1024)} fusion(f32[1024,16384]{1,0:T(8,128)} %get-tuple-element.78, f32[16384]{0:T(1024)} %subtract_reduce_fusion.2, f32[1024]{0:T(1024)S(1)} %negate_add_fusion), kind=kLoop, calls=%fused_computation.10 | loop fusion | flops 50315264 | bytes 67244032 | tf_op jit(solution)/shard_map/reduce_sum | solution.py:25
  430.5 21.0 %subtract_reduce_fusion.1 = f32[1024]{0:T(1024)S(1)} fusion(f32[1024,16384]{1,0:T(8,128)} %get-tuple-element.78, f32[16384]{0:T(1024)S(1)} %all_gather.14), kind=kLoop, calls=%fused_computation.16 | loop fusion | flops 50330624 | bytes 67178496 | tf_op jit(solution)/shard_map/reduce_max | solution.py:42
  451.5 19.1 %pmax.23 = f32[1024]{0:T(1024)S(1)} all-reduce(f32[1024]{0:T(1024)S(1)} %subtract_reduce_fusion.1), channel_id=1, replica_groups=mesh['samp'=8,'state'=4] {'samp'}, use_global_device_ids=true, to_apply=%region_21.0 | all-reduce | flops 1024 | bytes 8192 | tf_op jit(solution)/shard_map/pmax | solution.py:42
  470.7 21.4 %exponential_reduce_fusion.1 = f32[1024]{0:T(1024)S(1)} fusion(f32[1024,16384]{1,0:T(8,128)} %get-tuple-element.78, f32[1024]{0:T(1024)S(1)} %pmax.23, f32[16384]{0:T(1024)S(1)} %all_gather.14), kind=kLoop, calls=%fused_computation.9 | loop fusion | flops 67107840 | bytes 67182592 | tf_op jit(solution)/shard_map/reduce_sum | solution.py:43
  492.1 17.1 %psum.37 = f32[1024]{0:T(1024)S(1)} all-reduce(f32[1024]{0:T(1024)S(1)} %exponential_reduce_fusion.1), channel_id=1, replica_groups=mesh['samp'=8,'state'=4] {'samp'}, use_global_device_ids=true, to_apply=%region_23.0 | all-reduce | flops 1024 | bytes 8192 | tf_op jit(solution)/shard_map/psum | solution.py:43
  509.2 21.5 %subtract_reduce_fusion = f32[16384]{0:T(1024)} fusion(f32[1024,16384]{1,0:T(8,128)} %get-tuple-element.78, f32[1024]{0:T(1024)S(1)} %get-tuple-element.126), kind=kLoop, calls=%fused_computation.15 | loop fusion | flops 33538048 | bytes 67178496 | tf_op jit(solution)/shard_map/reduce_max | solution.py:24
  534.1 167.1 %while.11 = (s32[]{:T(128)}, f32[32,512]{1,0:T(8,128)S(1)}, s32[32]{0:T(128)S(1)}, s32[16384]{0:T(1024)S(1)}, f32[1024]{0:T(1024)S(1)}, /*index=5*/bf16[1024,163...) while((s32[]{:T(128)}, f32[32,512]{1,0:T(8,128)S(1)}, ...), condition=%wide.region_27.0_spmd.clone, body=%wide.region_25.27_spmd.clone.sunk | while | flops 3145226 | bytes 5308661 | solution.py:71
  701.2 24.3 %exponential_reduce_fusion = f32[16384]{0:T(1024)} fusion(f32[1024,16384]{1,0:T(8,128)} %get-tuple-element.78, f32[16384]{0:T(1024)} %subtract_reduce_fusion, f32[1024]{0:T(1024)S(1)} %get-tuple-element.166), kind=kLoop, calls=%fused_computation.8 | loop fusion | flops 50315264 | bytes 67244032 | tf_op jit(solution)/shard_map/reduce_sum | solution.py:25
  727.3 8.5 %psum.38 = f32[]{:T(128)} all-reduce(f32[]{:T(128)} %bitcast.7), channel_id=1, replica_groups=mesh['samp'=8,'state'=4] {'state'}, use_global_device_ids=true, to_apply=%region_24.0 | all-reduce | flops 1 | bytes 8 | tf_op jit(solution)/shard_map/psum | solution.py:11
  748.5 8.5 %all-reduce.2.cloned.1.call-done = f32[16384]{0:T(1024)} async-done(((f32[16384]{0:T(1024)}), f32[16384]{0:T(1024)}) %all-reduce.2.cloned.1.call-update) | async-done | bytes 65552 | tf_op jit(solution)/shard_map/psum | solution.py:85
  (243 shorter events, 193.2 us)
Async XLA Ops:
  104.5 28.7 %all-to-all-start = ((f32[4,1,4096]{2,1,0:T(1,128)}), f32[4,1,4096]{2,1,0:T(1,128)S(1)}, u32[]{:S(2)}, u32[]{:S(2)}) async-start(f32[4,1,4096]{2,1,0:T(1,128)} %bitcast), calls=%async_computation | async-start | bytes 131072 | tf_op jit(solution)/shard_map/all_to_all | solution.py:28
  133.2 7.4 all-to-all-start.1
  146.0 81.7 %copy-start.2 = (s32[1024]{0:T(1024)S(1)}, s32[1024]{0:T(1024)}, u32[]{:S(2)}) copy-start(s32[1024]{0:T(1024)} %param.8) | copy-start | bytes 12292
  249.2 27.7 %all-to-all-start.2 = ((f32[4,1,4096]{2,1,0:T(1,128)}), f32[4,1,4096]{2,1,0:T(1,128)S(1)}, u32[]{:S(2)}, u32[]{:S(2)}) async-start(f32[4,1,4096]{2,1,0:T(1,128)} %bitcast.2), calls=%async_computation.2 | async-start | bytes 131072 | tf_op jit(solution)/shard_map/all_to_all | solution.py:28
  276.9 7.4 all-to-all-start.3
  368.5 52.6 %copy-start.1 = (s32[16384]{0:T(1024)S(1)}, s32[16384]{0:T(1024)}, u32[]{:S(2)}) copy-start(s32[16384]{0:T(1024)} %param.9) | copy-start | bytes 196612
  390.0 27.7 %all-to-all-start.4 = ((f32[4,1,4096]{2,1,0:T(1,128)}), f32[4,1,4096]{2,1,0:T(1,128)S(1)}, u32[]{:S(2)}, u32[]{:S(2)}) async-start(f32[4,1,4096]{2,1,0:T(1,128)} %bitcast.4), calls=%async_computation.4 | async-start | bytes 131072 | tf_op jit(solution)/shard_map/all_to_all | solution.py:28
  417.8 7.4 all-to-all-start.5
  470.7 63.4 %copy-start = (f32[1024,128]{1,0:T(8,128)S(1)}, f32[1024,128]{1,0:T(8,128)}, u32[]{:S(2)}) copy-start(f32[1024,128]{1,0:T(8,128)} %param.7) | copy-start | bytes 1572868
  530.7 205.0 %all-to-all-start.6 = ((f32[4,1,4096]{2,1,0:T(1,128)}), f32[4,1,4096]{2,1,0:T(1,128)S(1)}, u32[]{:S(2)}, u32[]{:S(2)}) async-start(f32[4,1,4096]{2,1,0:T(1,128)} %bitcast.8), calls=%async_computation.6 | async-start | bytes 131072 | tf_op jit(solution)/shard_map/all_to_all | solution.py:28
  534.0 223.0 %all-reduce.2.cloned.1.call-start = ((), (), s32[]{:S(2)}) async-start(), calls=%async_computation.8 | async-start | bytes 131072 | tf_op jit(solution)/shard_map/psum | solution.py:85
  735.8 7.4 all-to-all-start.7
Sparse Core Ops, SparseCore 0:
  726.3 30.6 all-reduce.1
where the time goes:
time: 768 us; the launch traced here: 765 us
  other arithmetic  423 us (55%)
  blocking collectives  141 us (18%)
  local copies, waits for them, and re-layouts  93.4 us (12%)
  loops' own time  42.3 us (6%)
  starting transfers between devices  27.3 us (4%)
  waiting for transfers between devices  23.3 us (3%)
  between operations  14.9 us (2%)
    reduce_max x4, other arithmetic, sample_denominator(): best = jnp.max(terms, axis=0)  139 us
    reduce_sum x4, other arithmetic, sample_denominator(): total = jnp.sum(jnp.exp(terms - best[None, :]), axis=0)  97.6 us
    reduce_sum x3, other arithmetic, state_update(): total = lax.psum(jnp.sum(jnp.exp(terms - best[:, None]), axis=1), 'samp')  64.2 us
    reduce_max x3, other arithmetic, state_update(): best = lax.pmax(jnp.max(terms, axis=1), 'samp')  63 us
    pmax x3, blocking collectives, state_update(): best = lax.pmax(jnp.max(terms, axis=1), 'samp')  60.6 us
    reduce_sum x32, other arithmetic, one(): return jnp.sum(jnp.where(match, lead[:, None] - energy_part, 0.0), axis=0)  54.7 us
    psum x3, blocking collectives, state_update(): total = lax.psum(jnp.sum(jnp.exp(terms - best[:, None]), axis=1), 'samp')  51.4 us
    another operation x1, loops' own time, own_terms_local(): return lax.map(one, jnp.arange(steps_count, dtype=jnp.int32)).reshape(width)  42.3 us
  transfers between devices with their start and end apart: 9, of which 5 were waited for; matrix products, arithmetic and copies ran while one was open for 29% of the time, Pallas kernels for 0%

commit v1 on v0

--- a/solution.py
+++ b/solution.py
@@ -40,7 +40,7 @@
 def state_update(energies, offsets, denom):
     terms = -local_energy(energies, offsets) - denom[None, :]
     best = lax.pmax(jnp.max(terms, axis=1), "samp")
-    total = lax.psum(jnp.sum(jnp.exp(terms - best[:, None]), axis=1), "samp")
+    total = jnp.sum(lax.all_gather(jnp.sum(jnp.exp(terms - best[:, None]), axis=1), "samp"), axis=0)
     return -(best + jnp.log(total))
 
 

time: 768 us -> 805 us (1.048)
  blocking collectives: 141 us -> 180 us
    all_gather x0 -> x3, blocking collectives: none -> 91.8 us  [state_update(): lax.all_gather(jnp.sum(jnp.exp(terms - best[:, None]), axis=1), 'samp')]
    psum x3 -> x0, blocking collectives: 51.4 us -> none  [state_update(): total = lax.psum(jnp.sum(jnp.exp(terms - best[:, None]), axis=1), 'samp')]
    reduce_sum x3 -> x6, other arithmetic: 64.2 us -> 64.2 us  [the longest x3 64.2 us: state_update(): jnp.sum(jnp.exp(terms - best[:, None]), axis=1)]
  transfers between devices with their start and end apart: 9 -> 9, of which waited for: 5 -> 5; matrix products, arithmetic and copies ran while one was open for 29% -> 28% of each run, Pallas kernels for 0% -> 0%
where the time goes in v1:
time: 805 us; the launch traced here: 802 us
  other arithmetic  423 us (53%)
  blocking collectives  180 us (22%)
  local copies, waits for them, and re-layouts  93.4 us (12%)
  loops' own time  42.3 us (5%)
  starting transfers between devices  27.3 us (3%)
  waiting for transfers between devices  21.9 us (3%)
  between operations  14.9 us (2%)
    reduce_max x4, other arithmetic, sample_denominator(): best = jnp.max(terms, axis=0)  139 us
    reduce_sum x4, other arithmetic, sample_denominator(): total = jnp.sum(jnp.exp(terms - best[None, :]), axis=0)  97.6 us
    all_gather x3, blocking collectives, state_update(): lax.all_gather(jnp.sum(jnp.exp(terms - best[:, None]), axis=1), 'samp')  91.8 us
    reduce_sum x3, other arithmetic, state_update(): jnp.sum(jnp.exp(terms - best[:, None]), axis=1)  64.2 us
    reduce_max x3, other arithmetic, state_update(): best = lax.pmax(jnp.max(terms, axis=1), 'samp')  63 us
    pmax x3, blocking collectives, state_update(): best = lax.pmax(jnp.max(terms, axis=1), 'samp')  58.6 us
    reduce_sum x32, other arithmetic, one(): return jnp.sum(jnp.where(match, lead[:, None] - energy_part, 0.0), axis=0)  54.7 us
    another operation x1, loops' own time, own_terms_local(): return lax.map(one, jnp.arange(steps_count, dtype=jnp.int32)).reshape(width)  42.3 us
  transfers between devices with their start and end apart: 9, of which 5 were waited for; matrix products, arithmetic and copies ran while one was open for 28% of the time, Pallas kernels for 0%

profile of v1, /device:TPU:0, one launch (start us, length us, event | category | flops | bytes accessed | tf_op | source)
XLA Modules:
  0.0 802.4 jit_solution(3402016208443005677)
XLA Ops:
  7.9 22.2 %add.42 = f32[1024,128,128]{2,1,0:T(8,128)} broadcast(f32[1024,128]{1,0:T(8,128)} %param.7), dimensions={0,1} | broadcast | bytes 67633152 | tf_op jit(solution)/shard_map/add | solution.py:18
  30.0 74.5 %subtract_reduce_fusion.6 = (f32[16384]{0:T(1024)}, f32[1024,16384]{1,0:T(8,128)}) fusion(f32[1024]{0:T(1024)S(1)} %convert_log_fusion, f32[128,8,128,128]{3,2,1,0:T(8,128)} %bitcast.23, bf16[1024,16384]{1,0:T(8,128)(2,1)} %param.6), kind=kLoop, calls=%fused_computation.21 | loop fusion | flops 67092480 | bytes 167841792 | tf_op jit(solution)/shard_map/reduce_max | solution.py:24
  108.8 24.4 %exponential_reduce_fusion.6 = f32[16384]{0:T(1024)} fusion(f32[1024,16384]{1,0:T(8,128)} %get-tuple-element.78, f32[16384]{0:T(1024)} %get-tuple-element.77, f32[1024]{0:T(1024)S(1)} %convert_log_fusion), kind=kLoop, calls=%fused_computation.14 | loop fusion | flops 50315264 | bytes 67244032 | tf_op jit(solution)/shard_map/reduce_sum | solution.py:25
  146.0 21.0 %subtract_reduce_fusion.5 = f32[1024]{0:T(1024)S(1)} fusion(f32[1024,16384]{1,0:T(8,128)} %get-tuple-element.78, f32[16384]{0:T(1024)S(1)} %all_gather.30), kind=kLoop, calls=%fused_computation.20 | loop fusion | flops 50330624 | bytes 67178496 | tf_op jit(solution)/shard_map/reduce_max | solution.py:42
  167.0 22.1 %pmax.21 = f32[1024]{0:T(1024)S(1)} all-reduce(f32[1024]{0:T(1024)S(1)} %subtract_reduce_fusion.5), channel_id=1, replica_groups=mesh['samp'=8,'state'=4] {'samp'}, use_global_device_ids=true, to_apply=%region_5.0 | all-reduce | flops 1024 | bytes 8192 | tf_op jit(solution)/shard_map/pmax | solution.py:42
  189.1 21.4 %exponential_reduce_fusion.5 = f32[1024]{0:T(1024)S(1)} fusion(f32[1024,16384]{1,0:T(8,128)} %get-tuple-element.78, f32[1024]{0:T(1024)S(1)} %pmax.21, f32[16384]{0:T(1024)S(1)} %all_gather.30), kind=kLoop, calls=%fused_computation.13 | loop fusion | flops 67107840 | bytes 67182592 | tf_op jit(solution)/shard_map/reduce_sum | solution.py:43
  210.5 30.6 %all-gather = f32[8192]{0:T(1024)S(1)} all-gather(f32[1024]{0:T(1024)S(1)} %exponential_reduce_fusion.5), channel_id=2, replica_groups=mesh['samp'=8,'state'=4] {'samp'}, dimensions={0}, use_global_device_ids=true | all-gather | bytes 36864 | tf_op jit(solution)/shard_map/all_gather | solution.py:43
  241.2 21.5 %subtract_reduce_fusion.4 = f32[16384]{0:T(1024)} fusion(f32[1024,16384]{1,0:T(8,128)} %get-tuple-element.78, f32[1024]{0:T(1024)S(1)} %negate_add_fusion.1), kind=kLoop, calls=%fused_computation.19 | loop fusion | flops 33538048 | bytes 67178496 | tf_op jit(solution)/shard_map/reduce_max | solution.py:24
  266.0 24.4 %exponential_reduce_fusion.4 = f32[16384]{0:T(1024)} fusion(f32[1024,16384]{1,0:T(8,128)} %get-tuple-element.78, f32[16384]{0:T(1024)} %subtract_reduce_fusion.4, f32[1024]{0:T(1024)S(1)} %negate_add_fusion.1), kind=kLoop, calls=%fused_computation.12 | loop fusion | flops 50315264 | bytes 67244032 | tf_op jit(solution)/shard_map/reduce_sum | solution.py:25
  303.2 21.0 %subtract_reduce_fusion.3 = f32[1024]{0:T(1024)S(1)} fusion(f32[1024,16384]{1,0:T(8,128)} %get-tuple-element.78, f32[16384]{0:T(1024)S(1)} %all_gather.33), kind=kLoop, calls=%fused_computation.18 | loop fusion | flops 50330624 | bytes 67178496 | tf_op jit(solution)/shard_map/reduce_max | solution.py:42
  324.2 17.3 %pmax.22 = f32[1024]{0:T(1024)S(1)} all-reduce(f32[1024]{0:T(1024)S(1)} %subtract_reduce_fusion.3), channel_id=1, replica_groups=mesh['samp'=8,'state'=4] {'samp'}, use_global_device_ids=true, to_apply=%region_13.0 | all-reduce | flops 1024 | bytes 8192 | tf_op jit(solution)/shard_map/pmax | solution.py:42
  341.5 21.4 %exponential_reduce_fusion.3 = f32[1024]{0:T(1024)S(1)} fusion(f32[1024,16384]{1,0:T(8,128)} %get-tuple-element.78, f32[1024]{0:T(1024)S(1)} %pmax.22, f32[16384]{0:T(1024)S(1)} %all_gather.33), kind=kLoop, calls=%fused_computation.11 | loop fusion | flops 67107840 | bytes 67182592 | tf_op jit(solution)/shard_map/reduce_sum | solution.py:43
  362.9 30.6 %all-gather.1 = f32[8192]{0:T(1024)S(1)} all-gather(f32[1024]{0:T(1024)S(1)} %exponential_reduce_fusion.3), channel_id=3, replica_groups=mesh['samp'=8,'state'=4] {'samp'}, dimensions={0}, use_global_device_ids=true | all-gather | bytes 36864 | tf_op jit(solution)/shard_map/all_gather | solution.py:43
  393.5 21.5 %subtract_reduce_fusion.2 = f32[16384]{0:T(1024)} fusion(f32[1024,16384]{1,0:T(8,128)} %get-tuple-element.78, f32[1024]{0:T(1024)S(1)} %negate_add_fusion), kind=kLoop, calls=%fused_computation.17 | loop fusion | flops 33538048 | bytes 67178496 | tf_op jit(solution)/shard_map/reduce_max | solution.py:24
  418.3 24.4 %exponential_reduce_fusion.2 = f32[16384]{0:T(1024)} fusion(f32[1024,16384]{1,0:T(8,128)} %get-tuple-element.78, f32[16384]{0:T(1024)} %subtract_reduce_fusion.2, f32[1024]{0:T(1024)S(1)} %negate_add_fusion), kind=kLoop, calls=%fused_computation.10 | loop fusion | flops 50315264 | bytes 67244032 | tf_op jit(solution)/shard_map/reduce_sum | solution.py:25
  455.5 21.0 %subtract_reduce_fusion.1 = f32[1024]{0:T(1024)S(1)} fusion(f32[1024,16384]{1,0:T(8,128)} %get-tuple-element.78, f32[16384]{0:T(1024)S(1)} %all_gather.36), kind=kLoop, calls=%fused_computation.16 | loop fusion | flops 50330624 | bytes 67178496 | tf_op jit(solution)/shard_map/reduce_max | solution.py:42
  476.5 19.1 %pmax.23 = f32[1024]{0:T(1024)S(1)} all-reduce(f32[1024]{0:T(1024)S(1)} %subtract_reduce_fusion.1), channel_id=1, replica_groups=mesh['samp'=8,'state'=4] {'samp'}, use_global_device_ids=true, to_apply=%region_21.0 | all-reduce | flops 1024 | bytes 8192 | tf_op jit(solution)/shard_map/pmax | solution.py:42
  495.7 21.4 %exponential_reduce_fusion.1 = f32[1024]{0:T(1024)S(1)} fusion(f32[1024,16384]{1,0:T(8,128)} %get-tuple-element.78, f32[1024]{0:T(1024)S(1)} %pmax.23, f32[16384]{0:T(1024)S(1)} %all_gather.36), kind=kLoop, calls=%fused_computation.9 | loop fusion | flops 67107840 | bytes 67182592 | tf_op jit(solution)/shard_map/reduce_sum | solution.py:43
  517.1 30.6 %all-gather.2 = f32[8192]{0:T(1024)S(1)} all-gather(f32[1024]{0:T(1024)S(1)} %exponential_reduce_fusion.1), channel_id=4, replica_groups=mesh['samp'=8,'state'=4] {'samp'}, dimensions={0}, use_global_device_ids=true | all-gather | bytes 36864 | tf_op jit(solution)/shard_map/all_gather | solution.py:43
  547.8 21.5 %subtract_reduce_fusion = f32[16384]{0:T(1024)} fusion(f32[1024,16384]{1,0:T(8,128)} %get-tuple-element.78, f32[1024]{0:T(1024)S(1)} %get-tuple-element.126), kind=kLoop, calls=%fused_computation.15 | loop fusion | flops 33538048 | bytes 67178496 | tf_op jit(solution)/shard_map/reduce_max | solution.py:24
  572.6 167.0 %while.11 = (s32[]{:T(128)}, f32[32,512]{1,0:T(8,128)S(1)}, s32[32]{0:T(128)S(1)}, s32[16384]{0:T(1024)S(1)}, f32[1024]{0:T(1024)S(1)}, /*index=5*/bf16[1024,163...) while((s32[]{:T(128)}, f32[32,512]{1,0:T(8,128)S(1)}, ...), condition=%wide.region_27.0_spmd.clone, body=%wide.region_25.27_spmd.clone.sunk | while | flops 3145226 | bytes 5308661 | solution.py:71
  739.7 24.3 %exponential_reduce_fusion = f32[16384]{0:T(1024)} fusion(f32[1024,16384]{1,0:T(8,128)} %get-tuple-element.78, f32[16384]{0:T(1024)} %subtract_reduce_fusion, f32[1024]{0:T(1024)S(1)} %get-tuple-element.166), kind=kLoop, calls=%fused_computation.8 | loop fusion | flops 50315264 | bytes 67244032 | tf_op jit(solution)/shard_map/reduce_sum | solution.py:25
  765.8 8.5 %psum.14 = f32[]{:T(128)} all-reduce(f32[]{:T(128)} %bitcast.7), channel_id=1, replica_groups=mesh['samp'=8,'state'=4] {'state'}, use_global_device_ids=true, to_apply=%region_24.0 | all-reduce | flops 1 | bytes 8 | tf_op jit(solution)/shard_map/psum | solution.py:11
  787.0 7.0 all-reduce.2.cloned.1.call-done
  (249 shorter events, 193.3 us)
Async XLA Ops:
  104.5 28.7 %all-to-all-start = ((f32[4,1,4096]{2,1,0:T(1,128)}), f32[4,1,4096]{2,1,0:T(1,128)S(1)}, u32[]{:S(2)}, u32[]{:S(2)}) async-start(f32[4,1,4096]{2,1,0:T(1,128)} %bitcast), calls=%async_computation | async-start | bytes 131072 | tf_op jit(solution)/shard_map/all_to_all | solution.py:28
  133.2 7.4 all-to-all-start.1
  146.0 95.2 %copy-start.2 = (s32[1024]{0:T(1024)S(1)}, s32[1024]{0:T(1024)}, u32[]{:S(2)}) copy-start(s32[1024]{0:T(1024)} %param.8) | copy-start | bytes 12292
  262.7 27.7 %all-to-all-start.2 = ((f32[4,1,4096]{2,1,0:T(1,128)}), f32[4,1,4096]{2,1,0:T(1,128)S(1)}, u32[]{:S(2)}, u32[]{:S(2)}) async-start(f32[4,1,4096]{2,1,0:T(1,128)} %bitcast.2), calls=%async_computation.2 | async-start | bytes 131072 | tf_op jit(solution)/shard_map/all_to_all | solution.py:28
  290.4 7.4 all-to-all-start.3
  393.5 52.6 %copy-start.1 = (s32[16384]{0:T(1024)S(1)}, s32[16384]{0:T(1024)}, u32[]{:S(2)}) copy-start(s32[16384]{0:T(1024)} %param.9) | copy-start | bytes 196612
  415.0 27.7 %all-to-all-start.4 = ((f32[4,1,4096]{2,1,0:T(1,128)}), f32[4,1,4096]{2,1,0:T(1,128)S(1)}, u32[]{:S(2)}, u32[]{:S(2)}) async-start(f32[4,1,4096]{2,1,0:T(1,128)} %bitcast.4), calls=%async_computation.4 | async-start | bytes 131072 | tf_op jit(solution)/shard_map/all_to_all | solution.py:28
  442.8 7.4 all-to-all-start.5
  495.7 76.9 %copy-start = (f32[1024,128]{1,0:T(8,128)S(1)}, f32[1024,128]{1,0:T(8,128)}, u32[]{:S(2)}) copy-start(f32[1024,128]{1,0:T(8,128)} %param.7) | copy-start | bytes 1572868
  569.3 205.0 %all-to-all-start.6 = ((f32[4,1,4096]{2,1,0:T(1,128)}), f32[4,1,4096]{2,1,0:T(1,128)S(1)}, u32[]{:S(2)}, u32[]{:S(2)}) async-start(f32[4,1,4096]{2,1,0:T(1,128)} %bitcast.8), calls=%async_computation.6 | async-start | bytes 131072 | tf_op jit(solution)/shard_map/all_to_all | solution.py:28
  572.6 221.5 %all-reduce.2.cloned.1.call-start = ((), (), s32[]{:S(2)}) async-start(), calls=%async_computation.8 | async-start | bytes 131072 | tf_op jit(solution)/shard_map/psum | solution.py:85
  774.3 7.4 all-to-all-start.7
Sparse Core Ops, SparseCore 0:
  764.8 29.2 all-reduce.1
